TPU v7x, 32 devices: a whole 2x2x4 slice. The times are simulated.
32 devices in a mesh: ctx: 16 (over z, x, core), head: 2 (over y).
Axes of the slice: x: 2, y: 2, z: 4, core: 2. Of those that a mesh axis runs over, the one named last changes fastest.
Arguments:
- queries: bfloat16 [4096, 4096], P('ctx', 'head')
- keys: bfloat16 [4096, 1024], P(('ctx', 'head'))
- values: bfloat16 [4096, 1024], P(('ctx', 'head')), may hold values from -6 to 6
- selected: int32 [32, 8, 3], P('ctx', 'head'), may hold values from 0 to 6, as said below
Outputs:
- attended: bfloat16 [4096, 4096], P('ctx', 'head')
Inputs may be any that keep to these rules, and one draw needn't show every extreme that they name: selected[t, g, :] names 3 different blocks of 512 positions that lie before the block of tile t; where fewer than 3 such blocks exist, the remaining entries equal the tile's own block and name nothing more.
All inputs are finite; a program needn't handle non-finite values.
Results may differ from a plain program's by a relative error of at most 0.0041.
Values may be sent and summed in bfloat16 or wider, within the bound.
No kernel may reach another device: no remote copies, remote signals or barrier semaphores. Data moves between devices by JAX's collectives and lax.ppermute only.
A program may use at most 64 MiB of HBM per device.

v0:
```python
import math
import jax
import jax.numpy as jnp
from jax import lax
from jax.sharding import PartitionSpec as P

HD = 128
QH = 32
KVH = 8
BLK = 512
TILE = 128
floor_value = -1e30


def body(queries, keys, values, selected):
    local_rows = queries.shape[0]
    group_count = KVH // lax.axis_size("head")
    per_group = QH // KVH
    score_scale = HD ** (-0.5)
    own_keys, own_values = (
        lax.all_to_all(keys, "head", split_axis=1, concat_axis=0, tiled=True),
        lax.all_to_all(values, "head", split_axis=1, concat_axis=0, tiled=True),
    )
    query_four = queries.reshape(local_rows, group_count, per_group, HD)
    offset = lax.axis_index("ctx") * local_rows
    query_pos = offset + jnp.arange(local_rows, dtype=jnp.int32)
    query_block = query_pos // BLK
    row_select = jnp.repeat(selected, TILE, axis=0)

    def attend(running, key_rows, value_rows, first_row):
        row_count = key_rows.shape[0]
        key_pos = first_row + jnp.arange(row_count, dtype=jnp.int32)
        key_block = key_pos // BLK
        own_part = (key_block[None, :] == query_block[:, None]) & (
            key_pos[None, :] <= query_pos[:, None]
        )
        picked = jnp.any(row_select[:, :, :, None] == key_block[None, None, None, :], axis=2)
        picked = picked & (key_block[None, None, :] != query_block[:, None, None])
        allowed = jnp.transpose(picked | own_part[:, None, :], (1, 0, 2))

        def compute(current):
            running_max, totals, accumulated = current
            scores = (
                jnp.einsum(
                    "qgjd,kgd->gjqk",
                    query_four,
                    key_rows.reshape(row_count, group_count, HD),
                    preferred_element_type=jnp.float32,
                )
                * score_scale
            )
            live_mask = allowed[:, None]
            row_top = jnp.max(jnp.where(live_mask, scores, floor_value), axis=-1)
            newest = jnp.maximum(running_max, row_top)
            weights = jnp.where(live_mask, jnp.exp(scores - newest[..., None]), 0.0)
            factor = jnp.exp(running_max - newest)
            totals = totals * factor + jnp.sum(weights, axis=-1)
            product = jnp.einsum(
                "gjqk,kgd->gjqd",
                weights.astype(jnp.bfloat16),
                value_rows.reshape(row_count, group_count, HD),
                preferred_element_type=jnp.float32,
            )
            accumulated = accumulated * factor[..., None] + product
            return (newest, totals, accumulated)

        def keep_running(current):
            return current

        needed = jnp.any(allowed)
        return lax.cond(needed, compute, keep_running, running)

    start_max = jnp.full((group_count, per_group, local_rows), floor_value, jnp.float32)
    start_totals = jnp.zeros((group_count, per_group, local_rows), jnp.float32)
    start_accumulated = jnp.zeros((group_count, per_group, local_rows, HD), jnp.float32)
    key_piece = lax.all_gather(own_keys, "ctx", axis=0, tiled=True)
    value_piece = lax.all_gather(own_values, "ctx", axis=0, tiled=True)
    row_count = key_piece.shape[0]
    step_rows = math.gcd(row_count, 512)

    def loop_body(block_index, current):
        key_part = lax.dynamic_slice_in_dim(key_piece, block_index * step_rows, step_rows, 0)
        value_part = lax.dynamic_slice_in_dim(value_piece, block_index * step_rows, step_rows, 0)
        return attend(current, key_part, value_part, block_index * step_rows)

    running_max, totals, accumulated = lax.fori_loop(
        0, row_count // step_rows, loop_body, (start_max, start_totals, start_accumulated)
    )
    mixed = accumulated / totals[..., None]
    return (
        jnp.transpose(mixed, (2, 0, 1, 3))
        .reshape(local_rows, group_count * per_group * HD)
        .astype(jnp.bfloat16)
    )


def solution(mesh):
    placed = (
        P("ctx", "head"),
        P(("ctx", "head"), None),
        P(("ctx", "head"), None),
        P("ctx", "head", None),
    )
    return jax.shard_map(
        body, mesh=mesh, in_specs=placed, out_specs=P("ctx", "head"), check_vma=False
    )
```

profile of v0, /device:TPU:27, one launch (start us, length us, event | category | flops | bytes accessed | tf_op | source)
XLA Modules:
  0.0 254.5 jit_solution(11256422979810992226)
XLA Ops:
  7.8 6.7 %all_to_all.38 = bf16[128,2,512]{0,2,1:T(8,128)(2,1)S(1)} all-to-all(bf16[128,2,512]{0,2,1:T(8,128)(2,1)S(1)} %bitcast.60), channel_id=1, replica_groups=mesh['ctx'=16,'head'=2] {'head'}, dimensions={1} | all-to-all | bytes 524288 | tf_op jit(solution)/shard_map/all_to_all | solution.py:21
  16.5 6.4 %all_to_all.39 = bf16[128,2,512]{0,2,1:T(8,128)(2,1)S(1)} all-to-all(bf16[128,2,512]{0,2,1:T(8,128)(2,1)S(1)} %bitcast.61), channel_id=1, replica_groups=mesh['ctx'=16,'head'=2] {'head'}, dimensions={1} | all-to-all | bytes 524288 | tf_op jit(solution)/shard_map/all_to_all | solution.py:22
  25.8 39.4 %all-gather.3.cloned.1.call-done = bf16[4096,512]{1,0:T(8,128)(2,1)} async-done(((bf16[256,512]{1,0:T(8,128)(2,1)}), bf16[4096,512]{1,0:T(8,128)(2,1)}) %all-gather.3.cloned.1.call-update) | async-done | bytes 4194320 | tf_op jit(solution)/shard_map/all_gather | solution.py:76
  65.2 6.4 %copy.69 = bf16[4096,512]{0,1:T(8,128)(2,1)} copy(bf16[4096,512]{1,0:T(8,128)(2,1)} %all-gather.3.cloned.1.call-done) | data formatting | bytes 8388608
  71.6 44.8 %all-gather.5.cloned.1.call-done = bf16[4096,512]{1,0:T(8,128)(2,1)} async-done(((bf16[256,512]{1,0:T(8,128)(2,1)}), bf16[4096,512]{1,0:T(8,128)(2,1)}) %all-gather.5.cloned.1.call-update) | async-done | bytes 4194320 | tf_op jit(solution)/shard_map/all_gather | solution.py:77
  116.4 6.5 %copy.71 = bf16[4096,512]{0,1:T(8,128)(2,1)} copy(bf16[4096,512]{1,0:T(8,128)(2,1)} %all-gather.5.cloned.1.call-done) | data formatting | bytes 8388608
  124.5 118.8 %while.21 = (s32[]{:T(128)}, f32[4,4,256]{2,1,0:T(4,128)S(1)}, f32[4,4,256]{2,1,0:T(4,128)S(1)}, f32[4,4,256,128]{3,2,1,0:T(8,128)}, bf16[4096,512]{0,1:T(8,128)...) while((s32[]{:T(128)}, f32[4,4,256]{2,1,0:T(4,128)S(1)}, ...), condition=%wide.region_7.8_spmd.clone.clone, body=%wide.region_0.7_spmd.clone.clone.sunk | while | flops 1103646720 | bytes 56711624 | solution.py:86
  128.2 11.1 %conditional.4 = ((f32[4,4,256]{2,1,0:T(4,128)S(1)}, f32[4,4,256]{2,1,0:T(4,128)S(1)}, f32[4,4,256,128]{3,2,1,0:T(8,128)})) conditional(s32[]{:T(128)} %convert_element_type.38, (f32[4,4,256]{2,1,0:T(4,128)S(1)}, f32[4,4,256]{2,1,0:T(4,128)S(1)}, f32[4,4,256,128]{3,2,1,0:T(8,128)}) %tuple.84, (pred[256,512]{0,1:T(8,128)(4,1)S(1)}, ...), branch_computations={%region_3.3_spmd, %region_4.6_spmd} | conditional | flops 1098915840 | bytes 54526076 | solution.py:71
  134.6 3.3 %multiply_add_fusion = f32[4,4,256,128]{3,2,1,0:T(8,128)S(1)} fusion(f32[4,4,256,128]{3,2,1,0:T(8,128)S(1)} %copy-done, bf16[512,4,128,1]{0,2,3,1:T(8,128)(2,1)S(1)} %bitcast.53, f32[4,512,256,4]{2,1,3,0:T(8,128)S(1)} %get-tuple-element.534, f32[4,4,256]{2,1,0:T(4,128)S(1)} %max.5, pred[4,256,512]{1,2,0:T(8,128)(4,1)S(1)} %and_or_fusion, ...), kind=kOutput, calls=%fused_computation.15 | convolution fusion | flops 546308096 | bytes 13664256 | tf_op jit(solution)/shard_map/while/body/eval_jaxpr/cond/branch_1_fun/gjqk,kgd->gjqd/dot_general | solution.py:58
  143.0 11.1 %conditional.4 = ((f32[4,4,256]{2,1,0:T(4,128)S(1)}, f32[4,4,256]{2,1,0:T(4,128)S(1)}, f32[4,4,256,128]{3,2,1,0:T(8,128)})) conditional(s32[]{:T(128)} %convert_element_type.38, (f32[4,4,256]{2,1,0:T(4,128)S(1)}, f32[4,4,256]{2,1,0:T(4,128)S(1)}, f32[4,4,256,128]{3,2,1,0:T(8,128)}) %tuple.84, (pred[256,512]{0,1:T(8,128)(4,1)S(1)}, ...), branch_computations={%region_3.3_spmd, %region_4.6_spmd} | conditional | flops 1098915840 | bytes 54526076 | solution.py:71
  149.5 3.3 %multiply_add_fusion = f32[4,4,256,128]{3,2,1,0:T(8,128)S(1)} fusion(f32[4,4,256,128]{3,2,1,0:T(8,128)S(1)} %copy-done, bf16[512,4,128,1]{0,2,3,1:T(8,128)(2,1)S(1)} %bitcast.53, f32[4,512,256,4]{2,1,3,0:T(8,128)S(1)} %get-tuple-element.534, f32[4,4,256]{2,1,0:T(4,128)S(1)} %max.5, pred[4,256,512]{1,2,0:T(8,128)(4,1)S(1)} %and_or_fusion, ...), kind=kOutput, calls=%fused_computation.15 | convolution fusion | flops 546308096 | bytes 13664256 | tf_op jit(solution)/shard_map/while/body/eval_jaxpr/cond/branch_1_fun/gjqk,kgd->gjqd/dot_general | solution.py:58
  157.9 11.1 %conditional.4 = ((f32[4,4,256]{2,1,0:T(4,128)S(1)}, f32[4,4,256]{2,1,0:T(4,128)S(1)}, f32[4,4,256,128]{3,2,1,0:T(8,128)})) conditional(s32[]{:T(128)} %convert_element_type.38, (f32[4,4,256]{2,1,0:T(4,128)S(1)}, f32[4,4,256]{2,1,0:T(4,128)S(1)}, f32[4,4,256,128]{3,2,1,0:T(8,128)}) %tuple.84, (pred[256,512]{0,1:T(8,128)(4,1)S(1)}, ...), branch_computations={%region_3.3_spmd, %region_4.6_spmd} | conditional | flops 1098915840 | bytes 54526076 | solution.py:71
  164.3 3.3 %multiply_add_fusion = f32[4,4,256,128]{3,2,1,0:T(8,128)S(1)} fusion(f32[4,4,256,128]{3,2,1,0:T(8,128)S(1)} %copy-done, bf16[512,4,128,1]{0,2,3,1:T(8,128)(2,1)S(1)} %bitcast.53, f32[4,512,256,4]{2,1,3,0:T(8,128)S(1)} %get-tuple-element.534, f32[4,4,256]{2,1,0:T(4,128)S(1)} %max.5, pred[4,256,512]{1,2,0:T(8,128)(4,1)S(1)} %and_or_fusion, ...), kind=kOutput, calls=%fused_computation.15 | convolution fusion | flops 546308096 | bytes 13664256 | tf_op jit(solution)/shard_map/while/body/eval_jaxpr/cond/branch_1_fun/gjqk,kgd->gjqd/dot_general | solution.py:58
  172.7 11.1 %conditional.4 = ((f32[4,4,256]{2,1,0:T(4,128)S(1)}, f32[4,4,256]{2,1,0:T(4,128)S(1)}, f32[4,4,256,128]{3,2,1,0:T(8,128)})) conditional(s32[]{:T(128)} %convert_element_type.38, (f32[4,4,256]{2,1,0:T(4,128)S(1)}, f32[4,4,256]{2,1,0:T(4,128)S(1)}, f32[4,4,256,128]{3,2,1,0:T(8,128)}) %tuple.84, (pred[256,512]{0,1:T(8,128)(4,1)S(1)}, ...), branch_computations={%region_3.3_spmd, %region_4.6_spmd} | conditional | flops 1098915840 | bytes 54526076 | solution.py:71
  179.2 3.3 %multiply_add_fusion = f32[4,4,256,128]{3,2,1,0:T(8,128)S(1)} fusion(f32[4,4,256,128]{3,2,1,0:T(8,128)S(1)} %copy-done, bf16[512,4,128,1]{0,2,3,1:T(8,128)(2,1)S(1)} %bitcast.53, f32[4,512,256,4]{2,1,3,0:T(8,128)S(1)} %get-tuple-element.534, f32[4,4,256]{2,1,0:T(4,128)S(1)} %max.5, pred[4,256,512]{1,2,0:T(8,128)(4,1)S(1)} %and_or_fusion, ...), kind=kOutput, calls=%fused_computation.15 | convolution fusion | flops 546308096 | bytes 13664256 | tf_op jit(solution)/shard_map/while/body/eval_jaxpr/cond/branch_1_fun/gjqk,kgd->gjqd/dot_general | solution.py:58
  187.6 11.1 %conditional.4 = ((f32[4,4,256]{2,1,0:T(4,128)S(1)}, f32[4,4,256]{2,1,0:T(4,128)S(1)}, f32[4,4,256,128]{3,2,1,0:T(8,128)})) conditional(s32[]{:T(128)} %convert_element_type.38, (f32[4,4,256]{2,1,0:T(4,128)S(1)}, f32[4,4,256]{2,1,0:T(4,128)S(1)}, f32[4,4,256,128]{3,2,1,0:T(8,128)}) %tuple.84, (pred[256,512]{0,1:T(8,128)(4,1)S(1)}, ...), branch_computations={%region_3.3_spmd, %region_4.6_spmd} | conditional | flops 1098915840 | bytes 54526076 | solution.py:71
  194.0 3.3 %multiply_add_fusion = f32[4,4,256,128]{3,2,1,0:T(8,128)S(1)} fusion(f32[4,4,256,128]{3,2,1,0:T(8,128)S(1)} %copy-done, bf16[512,4,128,1]{0,2,3,1:T(8,128)(2,1)S(1)} %bitcast.53, f32[4,512,256,4]{2,1,3,0:T(8,128)S(1)} %get-tuple-element.534, f32[4,4,256]{2,1,0:T(4,128)S(1)} %max.5, pred[4,256,512]{1,2,0:T(8,128)(4,1)S(1)} %and_or_fusion, ...), kind=kOutput, calls=%fused_computation.15 | convolution fusion | flops 546308096 | bytes 13664256 | tf_op jit(solution)/shard_map/while/body/eval_jaxpr/cond/branch_1_fun/gjqk,kgd->gjqd/dot_general | solution.py:58
  202.4 11.1 %conditional.4 = ((f32[4,4,256]{2,1,0:T(4,128)S(1)}, f32[4,4,256]{2,1,0:T(4,128)S(1)}, f32[4,4,256,128]{3,2,1,0:T(8,128)})) conditional(s32[]{:T(128)} %convert_element_type.38, (f32[4,4,256]{2,1,0:T(4,128)S(1)}, f32[4,4,256]{2,1,0:T(4,128)S(1)}, f32[4,4,256,128]{3,2,1,0:T(8,128)}) %tuple.84, (pred[256,512]{0,1:T(8,128)(4,1)S(1)}, ...), branch_computations={%region_3.3_spmd, %region_4.6_spmd} | conditional | flops 1098915840 | bytes 54526076 | solution.py:71
  208.9 3.3 %multiply_add_fusion = f32[4,4,256,128]{3,2,1,0:T(8,128)S(1)} fusion(f32[4,4,256,128]{3,2,1,0:T(8,128)S(1)} %copy-done, bf16[512,4,128,1]{0,2,3,1:T(8,128)(2,1)S(1)} %bitcast.53, f32[4,512,256,4]{2,1,3,0:T(8,128)S(1)} %get-tuple-element.534, f32[4,4,256]{2,1,0:T(4,128)S(1)} %max.5, pred[4,256,512]{1,2,0:T(8,128)(4,1)S(1)} %and_or_fusion, ...), kind=kOutput, calls=%fused_computation.15 | convolution fusion | flops 546308096 | bytes 13664256 | tf_op jit(solution)/shard_map/while/body/eval_jaxpr/cond/branch_1_fun/gjqk,kgd->gjqd/dot_general | solution.py:58
  217.3 11.1 %conditional.4 = ((f32[4,4,256]{2,1,0:T(4,128)S(1)}, f32[4,4,256]{2,1,0:T(4,128)S(1)}, f32[4,4,256,128]{3,2,1,0:T(8,128)})) conditional(s32[]{:T(128)} %convert_element_type.38, (f32[4,4,256]{2,1,0:T(4,128)S(1)}, f32[4,4,256]{2,1,0:T(4,128)S(1)}, f32[4,4,256,128]{3,2,1,0:T(8,128)}) %tuple.84, (pred[256,512]{0,1:T(8,128)(4,1)S(1)}, ...), branch_computations={%region_3.3_spmd, %region_4.6_spmd} | conditional | flops 1098915840 | bytes 54526076 | solution.py:71
  223.7 3.3 %multiply_add_fusion = f32[4,4,256,128]{3,2,1,0:T(8,128)S(1)} fusion(f32[4,4,256,128]{3,2,1,0:T(8,128)S(1)} %copy-done, bf16[512,4,128,1]{0,2,3,1:T(8,128)(2,1)S(1)} %bitcast.53, f32[4,512,256,4]{2,1,3,0:T(8,128)S(1)} %get-tuple-element.534, f32[4,4,256]{2,1,0:T(4,128)S(1)} %max.5, pred[4,256,512]{1,2,0:T(8,128)(4,1)S(1)} %and_or_fusion, ...), kind=kOutput, calls=%fused_computation.15 | convolution fusion | flops 546308096 | bytes 13664256 | tf_op jit(solution)/shard_map/while/body/eval_jaxpr/cond/branch_1_fun/gjqk,kgd->gjqd/dot_general | solution.py:58
  232.1 11.1 %conditional.4 = ((f32[4,4,256]{2,1,0:T(4,128)S(1)}, f32[4,4,256]{2,1,0:T(4,128)S(1)}, f32[4,4,256,128]{3,2,1,0:T(8,128)})) conditional(s32[]{:T(128)} %convert_element_type.38, (f32[4,4,256]{2,1,0:T(4,128)S(1)}, f32[4,4,256]{2,1,0:T(4,128)S(1)}, f32[4,4,256,128]{3,2,1,0:T(8,128)}) %tuple.84, (pred[256,512]{0,1:T(8,128)(4,1)S(1)}, ...), branch_computations={%region_3.3_spmd, %region_4.6_spmd} | conditional | flops 1098915840 | bytes 54526076 | solution.py:71
  238.6 3.3 %multiply_add_fusion = f32[4,4,256,128]{3,2,1,0:T(8,128)S(1)} fusion(f32[4,4,256,128]{3,2,1,0:T(8,128)S(1)} %copy-done, bf16[512,4,128,1]{0,2,3,1:T(8,128)(2,1)S(1)} %bitcast.53, f32[4,512,256,4]{2,1,3,0:T(8,128)S(1)} %get-tuple-element.534, f32[4,4,256]{2,1,0:T(4,128)S(1)} %max.5, pred[4,256,512]{1,2,0:T(8,128)(4,1)S(1)} %and_or_fusion, ...), kind=kOutput, calls=%fused_computation.15 | convolution fusion | flops 546308096 | bytes 13664256 | tf_op jit(solution)/shard_map/while/body/eval_jaxpr/cond/branch_1_fun/gjqk,kgd->gjqd/dot_general | solution.py:58
  243.3 1.9 fusion.24
  (194 shorter events, 96.1 us)
Async XLA Ops:
  6.5 18.1 %copy-start.2 = (bf16[256,2048]{1,0:T(8,128)(2,1)S(1)}, bf16[256,2048]{1,0:T(8,128)(2,1)}, u32[]{:S(2)}) copy-start(bf16[256,2048]{1,0:T(8,128)(2,1)} %param.8) | copy-start | bytes 3145732
  6.5 58.6 %all-gather.3.cloned.1.call-start = ((), (), s32[]{:S(2)}) async-start(), calls=%async_computation.2 | async-start | bytes 4456448 | tf_op jit(solution)/shard_map/all_gather | solution.py:76
  15.4 101.1 %all-gather.5.cloned.1.call-start = ((), (), s32[]{:S(2)}) async-start(), calls=%async_computation.3 | async-start | bytes 4456448 | tf_op jit(solution)/shard_map/all_gather | solution.py:77
  132.8 1.9 copy-start
  138.0 1.4 copy-start.1
  147.6 1.9 copy-start
  152.8 1.4 copy-start.1
  162.5 1.9 copy-start
  167.7 1.4 copy-start.1
  177.3 1.9 copy-start
  182.5 1.4 copy-start.1
  192.1 1.9 copy-start
  197.4 1.4 copy-start.1
  207.0 1.9 copy-start
  212.2 1.4 copy-start.1
  221.8 1.9 copy-start
  227.1 1.4 copy-start.1
  236.7 1.9 copy-start
  241.9 1.4 copy-start.1
Sparse Core Ops, SparseCore 0:
  15.5 49.6 all-gather.2
  67.3 49.0 all-gather.4
where the time goes:
time: 255 us; the launch traced here: 254 us
  waiting for transfers between devices  84.2 us (33%)
  local copies, waits for them, and re-layouts  56.3 us (22%)
  matrix products  41.6 us (16%)
  other arithmetic  39.5 us (15%)
  between operations  13.5 us (5%)
  blocking collectives  13.1 us (5%)
  loops' own time  6.12 us (2%)
    all_gather x1, waiting for transfers between devices, body(): value_piece = lax.all_gather(own_values, 'ctx', axis=0, tiled=True)  44.8 us
    all_gather x1, waiting for transfers between devices, body(): key_piece = lax.all_gather(own_keys, 'ctx', axis=0, tiled=True)  39.4 us
    dot_general x8, matrix products, compute(): jnp.einsum('gjqk,kgd->gjqd', weights.astype(jnp.bfloat16), value_rows.res...  26.6 us
    unnamed x9, local copies, waits for them, and re-layouts  17.2 us
    dot_general x8, matrix products, compute(): jnp.einsum('qgjd,kgd->gjqk', query_four, key_rows.reshape(row_count, grou...  15.1 us
    reduce_sum x8, other arithmetic, compute(): totals = totals * factor + jnp.sum(weights, axis=-1)  14.7 us
    cond x40, local copies, waits for them, and re-layouts  10.8 us
    dynamic_slice x8, local copies, waits for them, and re-layouts, loop_body(): lax.dynamic_slice_in_dim(value_piece, block_index * step_rows, step_rows, 0)  10.2 us
  transfers between devices with their start and end apart: 2, of which 2 were waited for; matrix products, arithmetic and copies ran while one was open for 4% of the time, Pallas kernels for 0%

commit v1 on v0

--- a/solution.py
+++ b/solution.py
@@ -10,6 +10,24 @@
 BLK = 512
 TILE = 128
 floor_value = -1e30
+
+
+def joined_along(pieces, dim):
+    pieces = jnp.moveaxis(pieces, 0, dim)
+    dims = pieces.shape
+    return pieces.reshape(*dims[:dim], dims[dim] * dims[dim + 1], *dims[dim + 2 :])
+
+
+def collected_by_bits(array, axis):
+    count = lax.axis_size(axis)
+    blocks = array[None]
+    for level in range(count.bit_length() - 1):
+        bit = 1 << level
+        other = lax.ppermute(blocks, axis, [(i, i ^ bit) for i in range(count)])
+        both = jnp.stack([blocks, other])
+        upper = lax.axis_index(axis) >> level & 1
+        blocks = jnp.where(upper == 0, both, both[::-1]).reshape(-1, *array.shape)
+    return blocks
 
 
 def body(queries, keys, values, selected):
@@ -74,7 +92,7 @@
     start_totals = jnp.zeros((group_count, per_group, local_rows), jnp.float32)
     start_accumulated = jnp.zeros((group_count, per_group, local_rows, HD), jnp.float32)
     key_piece = lax.all_gather(own_keys, "ctx", axis=0, tiled=True)
-    value_piece = lax.all_gather(own_values, "ctx", axis=0, tiled=True)
+    value_piece = joined_along(collected_by_bits(own_values, "ctx"), 0)
     row_count = key_piece.shape[0]
     step_rows = math.gcd(row_count, 512)
 

time: 255 us -> 325 us (1.27)
  waiting for transfers between devices: 84.2 us -> 142 us
  other arithmetic: 39.5 us -> 44.2 us
  local copies, waits for them, and re-layouts: 56.3 us -> 60.5 us
  starting transfers between devices: 0.04 us -> 3.6 us
    ppermute x0 -> x4, waiting for transfers between devices: none -> 142 us  [collected_by_bits(): other = lax.ppermute(blocks, axis, [(i, i ^ bit) for i in range(count)])]
    all_gather x1 -> x0, waiting for transfers between devices: 44.8 us -> none  [body(): value_piece = lax.all_gather(own_values, 'ctx', axis=0, tiled=True)]
    all_gather x1, waiting for transfers between devices: 39.4 us -> 0.01 us  [body(): key_piece = lax.all_gather(own_keys, 'ctx', axis=0, tiled=True)]
    ppermute x0 -> x4, starting transfers between devices: none -> 3.6 us  [collected_by_bits(): other = lax.ppermute(blocks, axis, [(i, i ^ bit) for i in range(count)])]
    another operation x8 -> x9, local copies, waits for them, and re-layouts: 7.71 us -> 10.8 us
    unnamed x9 -> x11, local copies, waits for them, and re-layouts: 17.2 us -> 15.9 us
  transfers between devices with their start and end apart: 2 -> 5, of which waited for: 2 -> 4; matrix products, arithmetic and copies ran while one was open for 4% -> 6% of each run, Pallas kernels for 0% -> 0%
where the time goes in v1:
time: 325 us; the launch traced here: 324 us
  waiting for transfers between devices  142 us (44%)
  local copies, waits for them, and re-layouts  60.5 us (19%)
  other arithmetic  44.2 us (14%)
  matrix products  41.6 us (13%)
  between operations  13.5 us (4%)
  blocking collectives  13.1 us (4%)
  loops' own time  5.54 us (2%)
  starting transfers between devices  3.6 us (1%)
    ppermute x4, waiting for transfers between devices, collected_by_bits(): other = lax.ppermute(blocks, axis, [(i, i ^ bit) for i in range(count)])  142 us
    dot_general x8, matrix products, compute(): jnp.einsum('gjqk,kgd->gjqd', weights.astype(jnp.bfloat16), value_rows.res...  26.6 us
    unnamed x11, local copies, waits for them, and re-layouts  15.9 us
    dot_general x8, matrix products, compute(): jnp.einsum('qgjd,kgd->gjqk', query_four, key_rows.reshape(row_count, grou...  15 us
    reduce_sum x8, other arithmetic, compute(): totals = totals * factor + jnp.sum(weights, axis=-1)  14.7 us
    cond x40, local copies, waits for them, and re-layouts  10.9 us
    dynamic_slice x8, local copies, waits for them, and re-layouts, loop_body(): lax.dynamic_slice_in_dim(value_piece, block_index * step_rows, step_rows, 0)  10.2 us
    reduce_or x8, other arithmetic, attend(): needed = jnp.any(allowed)  9.28 us
  transfers between devices with their start and end apart: 5, of which 4 were waited for; matrix products, arithmetic and copies ran while one was open for 6% of the time, Pallas kernels for 0%

profile of v1, /device:TPU:27, one launch (start us, length us, event | category | flops | bytes accessed | tf_op | source)
XLA Modules:
  0.0 323.8 jit_solution(16396191385157907401)
XLA Ops:
  7.7 6.7 %all_to_all.35 = bf16[128,2,512]{0,2,1:T(8,128)(2,1)S(1)} all-to-all(bf16[128,2,512]{0,2,1:T(8,128)(2,1)S(1)} %bitcast.83), channel_id=1, replica_groups=mesh['ctx'=16,'head'=2] {'head'}, dimensions={1} | all-to-all | bytes 524288 | tf_op jit(solution)/shard_map/all_to_all | solution.py:39
  16.4 6.4 %all_to_all.36 = bf16[128,2,512]{0,2,1:T(8,128)(2,1)S(1)} all-to-all(bf16[128,2,512]{0,2,1:T(8,128)(2,1)S(1)} %bitcast.84), channel_id=1, replica_groups=mesh['ctx'=16,'head'=2] {'head'}, dimensions={1} | all-to-all | bytes 524288 | tf_op jit(solution)/shard_map/all_to_all | solution.py:40
  27.6 12.9 %collective-permute-done.1 = bf16[2,256,512]{2,1,0:T(8,128)(2,1)S(1)} collective-permute-done((bf16[2,256,512]{2,1,0:T(8,128)(2,1)S(1)}, bf16[2,256,512]{2,1,0:T(8,128)(2,1)S(1)}, u32[]{:S(2)}, u32[]{:S(2)}) %collective-permute-start.1) | collective-permute-done | bytes 524320 | tf_op jit(solution)/shard_map/ppermute | solution.py:26
  41.1 40.1 %collective-permute-done.2 = bf16[4,256,512]{2,1,0:T(8,128)(2,1)S(1)} collective-permute-done((bf16[4,256,512]{2,1,0:T(8,128)(2,1)S(1)}, bf16[4,256,512]{2,1,0:T(8,128)(2,1)S(1)}, u32[]{:S(2)}, u32[]{:S(2)}) %collective-permute-start.2) | collective-permute-done | bytes 1048608 | tf_op jit(solution)/shard_map/ppermute | solution.py:26
  91.1 87.4 %collective-permute-done.3 = bf16[8,256,512]{1,0,2:T(8,128)(2,1)} collective-permute-done((bf16[8,256,512]{1,0,2:T(8,128)(2,1)}, bf16[8,256,512]{1,0,2:T(8,128)(2,1)}, u32[]{:S(2)}, u32[]{:S(2)}) %collective-permute-start.3) | collective-permute-done | bytes 2097184 | tf_op jit(solution)/shard_map/ppermute | solution.py:26
  182.4 4.2 %copy.104 = bf16[64,8,16,256]{3,1,2,0:T(8,128)(2,1)} copy(bf16[64,8,16,256]{3,2,1,0:T(8,128)(2,1)S(1)} %bitcast.72) | data formatting | bytes 8388608
  186.6 6.5 %copy.93 = bf16[4096,512]{0,1:T(8,128)(2,1)} copy(bf16[4096,512]{1,0:T(8,128)(2,1)} %all-gather.2.cloned.1.call-done) | data formatting | bytes 8388608
  194.7 117.9 %while.21 = (s32[]{:T(128)}, f32[4,4,256]{2,1,0:T(4,128)S(1)}, f32[4,4,256]{2,1,0:T(4,128)S(1)}, f32[4,4,256,128]{3,2,1,0:T(8,128)}, bf16[4096,512]{0,1:T(8,128)...) while((s32[]{:T(128)}, f32[4,4,256]{2,1,0:T(4,128)S(1)}, ...), condition=%wide.region_7.8_spmd.clone.clone, body=%wide.region_0.7_spmd.clone.clone.sunk | while | flops 1103646720 | bytes 56711624 | solution.py:104
  198.3 11.1 %conditional.4 = ((f32[4,4,256]{2,1,0:T(4,128)S(1)}, f32[4,4,256]{2,1,0:T(4,128)S(1)}, f32[4,4,256,128]{3,2,1,0:T(8,128)})) conditional(s32[]{:T(128)} %convert_element_type.38, (f32[4,4,256]{2,1,0:T(4,128)S(1)}, f32[4,4,256]{2,1,0:T(4,128)S(1)}, f32[4,4,256,128]{3,2,1,0:T(8,128)}) %tuple.86, (pred[256,512]{0,1:T(8,128)(4,1)S(1)}, ...), branch_computations={%region_3.3_spmd, %region_4.6_spmd} | conditional | flops 1098915840 | bytes 54526076 | solution.py:89
  204.7 3.3 %multiply_add_fusion = f32[4,4,256,128]{3,2,1,0:T(8,128)S(1)} fusion(f32[4,4,256,128]{3,2,1,0:T(8,128)S(1)} %copy-done, bf16[512,4,128,1]{0,2,3,1:T(8,128)(2,1)S(1)} %bitcast.73, f32[4,512,256,4]{2,1,3,0:T(8,128)S(1)} %get-tuple-element.543, f32[4,4,256]{2,1,0:T(4,128)S(1)} %max.5, pred[4,256,512]{1,2,0:T(8,128)(4,1)S(1)} %and_or_fusion, ...), kind=kOutput, calls=%fused_computation.15 | convolution fusion | flops 546308096 | bytes 13664256 | tf_op jit(solution)/shard_map/while/body/eval_jaxpr/cond/branch_1_fun/gjqk,kgd->gjqd/dot_general | solution.py:76
  213.0 11.1 %conditional.4 = ((f32[4,4,256]{2,1,0:T(4,128)S(1)}, f32[4,4,256]{2,1,0:T(4,128)S(1)}, f32[4,4,256,128]{3,2,1,0:T(8,128)})) conditional(s32[]{:T(128)} %convert_element_type.38, (f32[4,4,256]{2,1,0:T(4,128)S(1)}, f32[4,4,256]{2,1,0:T(4,128)S(1)}, f32[4,4,256,128]{3,2,1,0:T(8,128)}) %tuple.86, (pred[256,512]{0,1:T(8,128)(4,1)S(1)}, ...), branch_computations={%region_3.3_spmd, %region_4.6_spmd} | conditional | flops 1098915840 | bytes 54526076 | solution.py:89
  219.5 3.3 %multiply_add_fusion = f32[4,4,256,128]{3,2,1,0:T(8,128)S(1)} fusion(f32[4,4,256,128]{3,2,1,0:T(8,128)S(1)} %copy-done, bf16[512,4,128,1]{0,2,3,1:T(8,128)(2,1)S(1)} %bitcast.73, f32[4,512,256,4]{2,1,3,0:T(8,128)S(1)} %get-tuple-element.543, f32[4,4,256]{2,1,0:T(4,128)S(1)} %max.5, pred[4,256,512]{1,2,0:T(8,128)(4,1)S(1)} %and_or_fusion, ...), kind=kOutput, calls=%fused_computation.15 | convolution fusion | flops 546308096 | bytes 13664256 | tf_op jit(solution)/shard_map/while/body/eval_jaxpr/cond/branch_1_fun/gjqk,kgd->gjqd/dot_general | solution.py:76
  227.8 11.1 %conditional.4 = ((f32[4,4,256]{2,1,0:T(4,128)S(1)}, f32[4,4,256]{2,1,0:T(4,128)S(1)}, f32[4,4,256,128]{3,2,1,0:T(8,128)})) conditional(s32[]{:T(128)} %convert_element_type.38, (f32[4,4,256]{2,1,0:T(4,128)S(1)}, f32[4,4,256]{2,1,0:T(4,128)S(1)}, f32[4,4,256,128]{3,2,1,0:T(8,128)}) %tuple.86, (pred[256,512]{0,1:T(8,128)(4,1)S(1)}, ...), branch_computations={%region_3.3_spmd, %region_4.6_spmd} | conditional | flops 1098915840 | bytes 54526076 | solution.py:89
  234.2 3.3 %multiply_add_fusion = f32[4,4,256,128]{3,2,1,0:T(8,128)S(1)} fusion(f32[4,4,256,128]{3,2,1,0:T(8,128)S(1)} %copy-done, bf16[512,4,128,1]{0,2,3,1:T(8,128)(2,1)S(1)} %bitcast.73, f32[4,512,256,4]{2,1,3,0:T(8,128)S(1)} %get-tuple-element.543, f32[4,4,256]{2,1,0:T(4,128)S(1)} %max.5, pred[4,256,512]{1,2,0:T(8,128)(4,1)S(1)} %and_or_fusion, ...), kind=kOutput, calls=%fused_computation.15 | convolution fusion | flops 546308096 | bytes 13664256 | tf_op jit(solution)/shard_map/while/body/eval_jaxpr/cond/branch_1_fun/gjqk,kgd->gjqd/dot_general | solution.py:76
  242.5 11.1 %conditional.4 = ((f32[4,4,256]{2,1,0:T(4,128)S(1)}, f32[4,4,256]{2,1,0:T(4,128)S(1)}, f32[4,4,256,128]{3,2,1,0:T(8,128)})) conditional(s32[]{:T(128)} %convert_element_type.38, (f32[4,4,256]{2,1,0:T(4,128)S(1)}, f32[4,4,256]{2,1,0:T(4,128)S(1)}, f32[4,4,256,128]{3,2,1,0:T(8,128)}) %tuple.86, (pred[256,512]{0,1:T(8,128)(4,1)S(1)}, ...), branch_computations={%region_3.3_spmd, %region_4.6_spmd} | conditional | flops 1098915840 | bytes 54526076 | solution.py:89
  248.9 3.3 %multiply_add_fusion = f32[4,4,256,128]{3,2,1,0:T(8,128)S(1)} fusion(f32[4,4,256,128]{3,2,1,0:T(8,128)S(1)} %copy-done, bf16[512,4,128,1]{0,2,3,1:T(8,128)(2,1)S(1)} %bitcast.73, f32[4,512,256,4]{2,1,3,0:T(8,128)S(1)} %get-tuple-element.543, f32[4,4,256]{2,1,0:T(4,128)S(1)} %max.5, pred[4,256,512]{1,2,0:T(8,128)(4,1)S(1)} %and_or_fusion, ...), kind=kOutput, calls=%fused_computation.15 | convolution fusion | flops 546308096 | bytes 13664256 | tf_op jit(solution)/shard_map/while/body/eval_jaxpr/cond/branch_1_fun/gjqk,kgd->gjqd/dot_general | solution.py:76
  257.2 11.1 %conditional.4 = ((f32[4,4,256]{2,1,0:T(4,128)S(1)}, f32[4,4,256]{2,1,0:T(4,128)S(1)}, f32[4,4,256,128]{3,2,1,0:T(8,128)})) conditional(s32[]{:T(128)} %convert_element_type.38, (f32[4,4,256]{2,1,0:T(4,128)S(1)}, f32[4,4,256]{2,1,0:T(4,128)S(1)}, f32[4,4,256,128]{3,2,1,0:T(8,128)}) %tuple.86, (pred[256,512]{0,1:T(8,128)(4,1)S(1)}, ...), branch_computations={%region_3.3_spmd, %region_4.6_spmd} | conditional | flops 1098915840 | bytes 54526076 | solution.py:89
  263.7 3.3 %multiply_add_fusion = f32[4,4,256,128]{3,2,1,0:T(8,128)S(1)} fusion(f32[4,4,256,128]{3,2,1,0:T(8,128)S(1)} %copy-done, bf16[512,4,128,1]{0,2,3,1:T(8,128)(2,1)S(1)} %bitcast.73, f32[4,512,256,4]{2,1,3,0:T(8,128)S(1)} %get-tuple-element.543, f32[4,4,256]{2,1,0:T(4,128)S(1)} %max.5, pred[4,256,512]{1,2,0:T(8,128)(4,1)S(1)} %and_or_fusion, ...), kind=kOutput, calls=%fused_computation.15 | convolution fusion | flops 546308096 | bytes 13664256 | tf_op jit(solution)/shard_map/while/body/eval_jaxpr/cond/branch_1_fun/gjqk,kgd->gjqd/dot_general | solution.py:76
  272.0 11.1 %conditional.4 = ((f32[4,4,256]{2,1,0:T(4,128)S(1)}, f32[4,4,256]{2,1,0:T(4,128)S(1)}, f32[4,4,256,128]{3,2,1,0:T(8,128)})) conditional(s32[]{:T(128)} %convert_element_type.38, (f32[4,4,256]{2,1,0:T(4,128)S(1)}, f32[4,4,256]{2,1,0:T(4,128)S(1)}, f32[4,4,256,128]{3,2,1,0:T(8,128)}) %tuple.86, (pred[256,512]{0,1:T(8,128)(4,1)S(1)}, ...), branch_computations={%region_3.3_spmd, %region_4.6_spmd} | conditional | flops 1098915840 | bytes 54526076 | solution.py:89
  278.4 3.3 %multiply_add_fusion = f32[4,4,256,128]{3,2,1,0:T(8,128)S(1)} fusion(f32[4,4,256,128]{3,2,1,0:T(8,128)S(1)} %copy-done, bf16[512,4,128,1]{0,2,3,1:T(8,128)(2,1)S(1)} %bitcast.73, f32[4,512,256,4]{2,1,3,0:T(8,128)S(1)} %get-tuple-element.543, f32[4,4,256]{2,1,0:T(4,128)S(1)} %max.5, pred[4,256,512]{1,2,0:T(8,128)(4,1)S(1)} %and_or_fusion, ...), kind=kOutput, calls=%fused_computation.15 | convolution fusion | flops 546308096 | bytes 13664256 | tf_op jit(solution)/shard_map/while/body/eval_jaxpr/cond/branch_1_fun/gjqk,kgd->gjqd/dot_general | solution.py:76
  286.7 11.1 %conditional.4 = ((f32[4,4,256]{2,1,0:T(4,128)S(1)}, f32[4,4,256]{2,1,0:T(4,128)S(1)}, f32[4,4,256,128]{3,2,1,0:T(8,128)})) conditional(s32[]{:T(128)} %convert_element_type.38, (f32[4,4,256]{2,1,0:T(4,128)S(1)}, f32[4,4,256]{2,1,0:T(4,128)S(1)}, f32[4,4,256,128]{3,2,1,0:T(8,128)}) %tuple.86, (pred[256,512]{0,1:T(8,128)(4,1)S(1)}, ...), branch_computations={%region_3.3_spmd, %region_4.6_spmd} | conditional | flops 1098915840 | bytes 54526076 | solution.py:89
  293.2 3.3 %multiply_add_fusion = f32[4,4,256,128]{3,2,1,0:T(8,128)S(1)} fusion(f32[4,4,256,128]{3,2,1,0:T(8,128)S(1)} %copy-done, bf16[512,4,128,1]{0,2,3,1:T(8,128)(2,1)S(1)} %bitcast.73, f32[4,512,256,4]{2,1,3,0:T(8,128)S(1)} %get-tuple-element.543, f32[4,4,256]{2,1,0:T(4,128)S(1)} %max.5, pred[4,256,512]{1,2,0:T(8,128)(4,1)S(1)} %and_or_fusion, ...), kind=kOutput, calls=%fused_computation.15 | convolution fusion | flops 546308096 | bytes 13664256 | tf_op jit(solution)/shard_map/while/body/eval_jaxpr/cond/branch_1_fun/gjqk,kgd->gjqd/dot_general | solution.py:76
  301.4 11.1 %conditional.4 = ((f32[4,4,256]{2,1,0:T(4,128)S(1)}, f32[4,4,256]{2,1,0:T(4,128)S(1)}, f32[4,4,256,128]{3,2,1,0:T(8,128)})) conditional(s32[]{:T(128)} %convert_element_type.38, (f32[4,4,256]{2,1,0:T(4,128)S(1)}, f32[4,4,256]{2,1,0:T(4,128)S(1)}, f32[4,4,256,128]{3,2,1,0:T(8,128)}) %tuple.86, (pred[256,512]{0,1:T(8,128)(4,1)S(1)}, ...), branch_computations={%region_3.3_spmd, %region_4.6_spmd} | conditional | flops 1098915840 | bytes 54526076 | solution.py:89
  307.9 3.3 %multiply_add_fusion = f32[4,4,256,128]{3,2,1,0:T(8,128)S(1)} fusion(f32[4,4,256,128]{3,2,1,0:T(8,128)S(1)} %copy-done, bf16[512,4,128,1]{0,2,3,1:T(8,128)(2,1)S(1)} %bitcast.73, f32[4,512,256,4]{2,1,3,0:T(8,128)S(1)} %get-tuple-element.543, f32[4,4,256]{2,1,0:T(4,128)S(1)} %max.5, pred[4,256,512]{1,2,0:T(8,128)(4,1)S(1)} %and_or_fusion, ...), kind=kOutput, calls=%fused_computation.15 | convolution fusion | flops 546308096 | bytes 13664256 | tf_op jit(solution)/shard_map/while/body/eval_jaxpr/cond/branch_1_fun/gjqk,kgd->gjqd/dot_general | solution.py:76
  (211 shorter events, 113.9 us)
Async XLA Ops:
  6.5 180.1 %all-gather.2.cloned.1.call-start = ((), (), s32[]{:S(2)}) async-start(), calls=%async_computation.2 | async-start | bytes 4456448 | tf_op jit(solution)/shard_map/all_gather | solution.py:94
  23.0 4.2 %collective-permute-start = (bf16[1,256,512]{2,1,0:T(8,128)(2,1)S(1)}, bf16[1,256,512]{2,1,0:T(8,128)(2,1)S(1)}, u32[]{:S(2)}, u32[]{:S(2)}) collective-permute-start(bf16[1,256,512]{2,1,0:T(8,128)(2,1)S(1)} %bitcast.85), channel_id=1, source_target_pairs={{0,2},{2,0},{4,6},{6,4},{8,10},{10,8},{12,14},{14,12},{16,18},{18,... | collective-permute-start | bytes 786440 | tf_op jit(solution)/shard_map/ppermute | solution.py:26
  27.3 13.2 %collective-permute-start.1 = (bf16[2,256,512]{2,1,0:T(8,128)(2,1)S(1)}, bf16[2,256,512]{2,1,0:T(8,128)(2,1)S(1)}, u32[]{:S(2)}, u32[]{:S(2)}) collective-permute-start(bf16[2,256,512]{2,1,0:T(8,128)(2,1)S(1)} %get-tuple-element.553), channel_id=1, source_target_pairs={{0,4},{2,6},{4,0},{6,2},{8,12},{10,14},{12,8},{14,10},{16,20},{18,... | collective-permute-start | bytes 1572872 | tf_op jit(solution)/shard_map/ppermute | solution.py:26
  40.8 40.4 %collective-permute-start.2 = (bf16[4,256,512]{2,1,0:T(8,128)(2,1)S(1)}, bf16[4,256,512]{2,1,0:T(8,128)(2,1)S(1)}, u32[]{:S(2)}, u32[]{:S(2)}) collective-permute-start(bf16[4,256,512]{2,1,0:T(8,128)(2,1)S(1)} %bitcast.77), channel_id=1, source_target_pairs={{0,8},{2,10},{4,12},{6,14},{8,0},{10,2},{12,4},{14,6},{16,24},{18,... | collective-permute-start | bytes 3145736 | tf_op jit(solution)/shard_map/ppermute | solution.py:26
  81.4 3.6 %copy-start.3 = (s32[2,4,3]{1,0,2:T(2,128)S(1)}, s32[2,4,3]{1,0,2:T(2,128)}, u32[]{:S(2)}) copy-start(s32[2,4,3]{1,0,2:T(2,128)} %param.11) | copy-start | bytes 292
  81.4 3.7 %copy-start.2 = (bf16[256,2048]{1,0:T(8,128)(2,1)S(1)}, bf16[256,2048]{1,0:T(8,128)(2,1)}, u32[]{:S(2)}) copy-start(bf16[256,2048]{1,0:T(8,128)(2,1)} %param.8) | copy-start | bytes 3145732
  84.9 93.6 %collective-permute-start.3 = (bf16[8,256,512]{1,0,2:T(8,128)(2,1)}, bf16[8,256,512]{1,0,2:T(8,128)(2,1)}, u32[]{:S(2)}, u32[]{:S(2)}) collective-permute-start(bf16[8,256,512]{1,0,2:T(8,128)(2,1)} %copy.91), channel_id=1, source_target_pairs={{0,16},{2,18},{4,20},{6,22},{8,24},{10,26},{12,28},{14,30},{16,0},... | collective-permute-start | bytes 6291464 | tf_op jit(solution)/shard_map/ppermute | solution.py:26
  202.8 1.9 copy-start
  208.1 1.4 copy-start.1
  217.6 1.9 copy-start
  222.8 1.4 copy-start.1
  232.3 1.9 copy-start
  237.5 1.4 copy-start.1
  247.1 1.9 copy-start
  252.3 1.4 copy-start.1
  261.8 1.9 copy-start
  267.0 1.4 copy-start.1
  276.5 1.9 copy-start
  281.7 1.4 copy-start.1
  291.3 1.9 copy-start
  296.5 1.4 copy-start.1
  306.0 1.9 copy-start
  311.2 1.4 copy-start.1
Sparse Core Ops, SparseCore 0:
  15.4 63.6 all-gather.1
